TPU v7x, 32 devices: a whole 2x2x4 slice. The times are simulated.
32 devices in a mesh: grp: 4 (over x, core), tp: 4 (over z), cores: 2 (over y).
Axes of the slice: x: 2, y: 2, z: 4, core: 2. Of those that a mesh axis runs over, the one named last changes fastest.
Arguments:
- tokens: bfloat16 [4096, 8192], P('grp', ('tp', 'cores')), may hold values from -6 to 6
- gate_up_weight: bfloat16 [8192, 2, 16384], P(None, None, ('tp', 'cores')), may hold values from -0.0625 to 0.0625
- down_factor_pool: bfloat16 [8, 8192, 256], P(('tp', 'cores'), 'grp'), may hold values from -0.0625 to 0.0625
- up_factor_pool: bfloat16 [8, 4, 8, 128, 1024], P(('tp', 'cores'), 'grp'), may hold values from -0.5 to 0.5
- segment_adapters: int32 [4, 3], replicated, may hold values from 0 to 7
- segment_tile_counts: int32 [4, 3], P('grp'), may hold values from 1 to 4, 8 in all within a row
- adapter_pool_rows: int32 [8], replicated, may hold values from 0 to 7, each once
Outputs:
- hidden: bfloat16 [4096, 16384], P('grp', ('tp', 'cores'))
Inputs may be any that keep to these rules, and one draw needn't show every extreme that they name: `segment_tile_counts`: each row sums to 8. `adapter_pool_rows`: each pool row appears once.
All inputs are finite; a program needn't handle non-finite values.
Results may differ from a plain program's by a relative error of at most 0.0036.
Values may be sent and summed in bfloat16 or wider, within the bound.
A program may use at most 320 MiB of HBM per device.

v0:
```python
import jax
import jax.numpy as jnp
from jax import lax
from jax.sharding import PartitionSpec as P

TILE = 128
adapter_scale = 0.5


def tile_segments(tile_lengths, tile_count):
    bounds = jnp.cumsum(tile_lengths)
    positions = jnp.arange(tile_count, dtype=jnp.int32)
    return jnp.sum((bounds[None, :] <= positions[:, None]).astype(jnp.int32), axis=1)


def per_device(
    tokens,
    gate_up_weight,
    down_factor_pool,
    up_factor_pool,
    segment_adapters,
    segment_tile_counts,
    adapter_pool_rows,
):
    groups = lax.axis_size("grp")
    device_shares = lax.axis_size(("tp", "cores"))
    piece_index = lax.axis_index(("tp", "cores"))
    token_count = tokens.shape[0]
    full_width = tokens.shape[1] * device_shares
    local_hidden_width = gate_up_weight.shape[2]
    twice_rank = down_factor_pool.shape[2]
    rank_size = twice_rank // 2
    share_rows = down_factor_pool.shape[1] // device_shares
    local_count = down_factor_pool.shape[0]
    seg_count = segment_adapters.shape[1]
    narrow = local_hidden_width // groups
    local_down_factor = down_factor_pool.reshape(
        local_count, device_shares, share_rows * twice_rank
    )
    local_up_factor = up_factor_pool.reshape(local_count, device_shares, -1)
    a_spread, b_spread = (
        lax.all_to_all(local_down_factor, ("tp", "cores"), split_axis=1, concat_axis=0, tiled=True),
        lax.all_to_all(local_up_factor, ("tp", "cores"), split_axis=1, concat_axis=0, tiled=True),
    )
    all_slots = jnp.take(adapter_pool_rows, segment_adapters)
    a_wanted = jnp.take(a_spread, all_slots, axis=0)
    b_wanted = jnp.take(b_spread, all_slots, axis=0)
    a_arrived, b_arrived = (
        lax.all_to_all(a_wanted, "grp", split_axis=0, concat_axis=2, tiled=True),
        lax.all_to_all(b_wanted, "grp", split_axis=0, concat_axis=2, tiled=True),
    )
    a_chosen = a_arrived.reshape(seg_count, groups, -1)
    b_chosen = b_arrived.reshape(seg_count, groups, -1)
    gathered = lax.all_gather(tokens, ("tp", "cores"), axis=1, tiled=True)
    frozen_output = jnp.dot(
        gathered,
        gate_up_weight.reshape(full_width, 2 * local_hidden_width),
        preferred_element_type=jnp.float32,
    )
    frozen_output = frozen_output.reshape(token_count, 2, local_hidden_width)
    tile_count = token_count // TILE
    tile_seg = tile_segments(segment_tile_counts[0], tile_count)
    a_tiles = jnp.take(a_chosen, tile_seg, axis=0).reshape(
        tile_count, groups * share_rows, twice_rank
    )
    own_features = lax.dynamic_slice_in_dim(
        gathered.reshape(token_count, groups, device_shares, share_rows), piece_index, 1, axis=2
    )
    own_features = own_features.reshape(tile_count, TILE, groups * share_rows)
    partial_shrink = jnp.einsum(
        "tkd,tdr->tkr", own_features, a_tiles, preferred_element_type=jnp.float32
    )
    reduced_input = lax.psum(partial_shrink, ("tp", "cores")).astype(jnp.bfloat16)
    b_tiles = jnp.take(b_chosen, tile_seg, axis=0).reshape(tile_count, groups, rank_size, 2, narrow)
    gate_adapter_delta = jnp.einsum(
        "tkr,tmrw->tkmw",
        reduced_input[:, :, :rank_size],
        b_tiles[:, :, :, 0, :],
        preferred_element_type=jnp.float32,
    )
    up_adapter_delta = jnp.einsum(
        "tkr,tmrw->tkmw",
        reduced_input[:, :, rank_size:],
        b_tiles[:, :, :, 1, :],
        preferred_element_type=jnp.float32,
    )
    gate_combined = frozen_output[:, 0, :] + adapter_scale * gate_adapter_delta.reshape(
        token_count, local_hidden_width
    )
    up_combined = frozen_output[:, 1, :] + adapter_scale * up_adapter_delta.reshape(
        token_count, local_hidden_width
    )
    return (jax.nn.silu(gate_combined) * up_combined).astype(jnp.bfloat16)


def solution(mesh):
    return jax.shard_map(
        per_device,
        mesh=mesh,
        in_specs=(
            P("grp", ("tp", "cores")),
            P(None, None, ("tp", "cores")),
            P(("tp", "cores"), "grp", None),
            P(("tp", "cores"), "grp", None, None, None),
            P(),
            P("grp", None),
            P(),
        ),
        out_specs=P("grp", ("tp", "cores")),
        check_vma=False,
    )
```

profile of v0, /device:TPU:0, one launch (start us, length us, event | category | flops | bytes accessed | tf_op | source)
XLA Modules:
  0.0 634.1 jit_solution(12954752661760870075)
XLA Ops:
  6.5 4.0 reshape.199
  11.1 7.3 %reduce.3 = bf16[8,65536]{1,0:T(8,128)(2,1)S(1)} reduce(bf16[8,1,65536]{2,1,0:T(2,128)(2,1)S(1)} %bitcast.106, bf16[]{:T(256)} %broadcast.154), dimensions={1}, to_apply=%bitcast.85.reduce_sub_computation | reduce | bytes 2097154
  18.4 1.9 reshape.206
  20.3 7.5 %all-to-all-start = ((bf16[8,2,32768]{2,1,0:T(2,128)(2,1)}), bf16[8,2,32768]{2,1,0:T(2,128)(2,1)S(1)}, u32[]{:S(2)}, u32[]{:S(2)}) async-start(bf16[8,2,32768]{2,1,0:T(2,128)(2,1)} %reshape.206), calls=%async_computation | async-start | bytes 2097152 | tf_op jit(solution)/shard_map/all_to_all | solution.py:42
  28.8 4.1 reshape.200
  32.9 13.0 %reduce.2 = bf16[8,131072]{1,0:T(8,128)(2,1)S(1)} reduce(bf16[8,1,131072]{2,1,0:T(2,128)(2,1)} %bitcast.100, bf16[]{:T(256)} %broadcast.154), dimensions={1}, to_apply=%bitcast.83.reduce_sub_computation | reduce | bytes 4194306
  45.9 3.2 reshape.204
  49.1 4.4 all-to-all-done
  54.5 3.6 all-to-all-start.2
  58.1 5.8 reshape.207
  63.9 2.7 copy.81
  66.6 3.0 gather_fusion.1
  69.6 4.2 reshape.131
  73.8 3.9 select_bitcast_fusion
  77.6 28.9 %all-to-all-done.2 = bf16[8,2,65536]{2,1,0:T(2,128)(2,1)S(1)} async-done(((bf16[8,2,65536]{2,1,0:T(2,128)(2,1)}), bf16[8,2,65536]{2,1,0:T(2,128)(2,1)S(1)}, u32[]{:S(2)}, u32[]{:S(2)}) %all-to-all-start.2) | async-done | bytes 2097184 | tf_op jit(solution)/shard_map/all_to_all | solution.py:43
  106.5 4.7 all-to-all-start.1
  111.2 4.3 reshape.205
  115.5 4.5 copy.79
  120.2 3.0 gather_fusion.3
  123.1 4.2 reshape.149
  128.9 2.6 reshape.159
  131.6 5.8 fusion.8
  137.3 5.0 all-to-all-start.3
  143.2 45.1 %copy.69 = bf16[1024,8,2,2048]{3,1,2,0:T(8,128)(2,1)} copy(bf16[1024,8,2,2048]{3,2,1,0:T(2,128)(2,1)} %bitcast.33) | data formatting | bytes 134217728
  188.3 83.4 %copy.48 = bf16[4096,8192]{1,0:T(8,128)(2,1)} copy(bf16[4096,8192]{0,1:T(8,128)(2,1)} %bitcast.1) | data formatting | bytes 134217728 | tf_op jit(solution)/shard_map/dot_general | solution.py:55
  271.8 3.1 copy.80
  274.9 5.4 gather_fusion.2
  280.3 7.9 %gather.27 = bf16[8,1024,256]{2,1,0:T(8,128)(2,1)} reshape(bf16[8,4,65536]{2,1,0:T(4,128)(2,1)} %gather_fusion.2) | data formatting | bytes 8388608 | tf_op jit(solution)/shard_map/jit(_take)/gather | solution.py:63
  288.3 5.2 copy.78
  294.5 5.4 gather_fusion.5
  299.9 5.5 gather_fusion.6
  305.4 8.3 %pad_maximum_fusion = bf16[8,4,131072]{2,1,0:T(4,128)(2,1)} fusion(bf16[8,4,65536]{2,1,0:T(4,128)(2,1)} %gather_fusion.6, bf16[8,4,65536]{2,1,0:T(4,128)(2,1)} %gather_fusion.5), kind=kLoop, calls=%fused_computation.15 | loop fusion | flops 16777216 | bytes 16777216
  313.8 12.5 %reshape.201 = bf16[8,4,128,2,512]{4,3,2,1,0:T(2,128)(2,1)} reshape(bf16[8,4,131072]{2,1,0:T(4,128)(2,1)} %pad_maximum_fusion) | data formatting | bytes 16777216 | tf_op jit(solution)/shard_map/jit(_take)/gather | solution.py:74
  326.3 8.2 %copy_select_fusion = bf16[8,4,128,2,512]{4,2,1,0,3:T(8,128)(2,1)} fusion(bf16[8,4,128,2,512]{4,3,2,1,0:T(2,128)(2,1)} %reshape.201, pred[8]{0:T(512)(128)(4,1)S(1)} %compare_and_fusion.1), kind=kLoop, calls=%fused_computation.16 | loop fusion | flops 4194304 | bytes 16777224 | tf_op jit(solution)/shard_map/jit(_take)/select_n | solution.py:74
  334.6 37.6 %all-gather.2.cloned.1.call-done = bf16[1024,8192]{1,0:T(8,128)(2,1)} async-done(((bf16[1024,1024]{1,0:T(8,128)(2,1)}), bf16[1024,8192]{1,0:T(8,128)(2,1)}) %all-gather.2.cloned.1.call-update) | async-done | bytes 16777232 | tf_op jit(solution)/shard_map/all_gather | solution.py:54
  372.2 10.3 %copy.70 = bf16[128,8,32,256]{3,2,1,0:T(8,128)(2,1)S(1)} copy(bf16[128,8,32,256]{3,1,2,0:T(8,128)(2,1)} %bitcast.102) | data formatting | bytes 33554432
  382.4 13.7 %dynamic-slice_reduce_fusion = bf16[1024,4,256]{2,1,0:T(4,128)(2,1)S(1)} fusion(bf16[1024,4,8,256]{3,2,1,0:T(8,128)(2,1)S(1)} %bitcast.98, s32[]{:T(128)S(6)} %select_n.80), kind=kLoop, calls=%fused_computation.27 | loop fusion | bytes 4194308 | tf_op jit(solution)/shard_map/dynamic_slice | solution.py:66
  396.1 2.7 reshape.202
  398.8 3.8 fusion.9
  402.6 70.0 %all-reduce.1 = bf16[8,128,256]{2,1,0:T(8,128)(2,1)S(1)} all-reduce(f32[8,128,256]{2,1,0:T(8,128)S(1)} %fusion.9), channel_id=1, replica_groups=mesh['grp'=4,'tp'=4,'cores'=2] {'tp','cores'}, use_global_device_ids=true, to_apply=%region_2.3 | all-reduce | flops 262144 | bytes 1572864 | tf_op jit(solution)/shard_map/psum | solution.py:73
  472.6 6.6 %broadcast_multiply_fusion.1 = f32[8,128,4,512]{3,1,2,0:T(8,128)} fusion(bf16[8,4,128,2,512]{4,2,1,0,3:T(8,128)(2,1)} %copy_select_fusion, bf16[8,128,256]{2,1,0:T(8,128)(2,1)S(1)} %all-reduce.1), kind=kOutput, calls=%fused_computation.24 | convolution fusion | flops 538968064 | bytes 12845056 | tf_op jit(solution)/shard_map/tkr,tmrw->tkmw/dot_general | solution.py:75
  479.2 6.6 %broadcast_multiply_fusion = f32[8,128,4,512]{3,1,2,0:T(8,128)} fusion(bf16[8,4,128,2,512]{4,2,1,0,3:T(8,128)(2,1)} %copy_select_fusion, bf16[8,128,256]{2,1,0:T(8,128)(2,1)S(1)} %all-reduce.1), kind=kOutput, calls=%fused_computation.23 | convolution fusion | flops 538968064 | bytes 12845056 | tf_op jit(solution)/shard_map/tkr,tmrw->tkmw/dot_general | solution.py:81
  485.8 12.1 %copy.60 = f32[8,128,4,512]{3,2,1,0:T(4,128)} copy(f32[8,128,4,512]{3,1,2,0:T(8,128)} %broadcast_multiply_fusion) | data formatting | bytes 16777216 | tf_op jit(solution)/shard_map/mul | solution.py:90
  497.9 11.1 %copy.72 = f32[128,8,4,512]{3,1,2,0:T(8,128)} copy(f32[128,8,4,512]{3,2,1,0:T(4,128)} %bitcast.94) | data formatting | bytes 16777216
  509.0 12.1 %copy.59 = f32[8,128,4,512]{3,2,1,0:T(4,128)} copy(f32[8,128,4,512]{3,1,2,0:T(8,128)} %broadcast_multiply_fusion.1) | data formatting | bytes 16777216 | tf_op jit(solution)/shard_map/mul | solution.py:87
  521.0 10.8 %copy.71 = f32[128,8,4,512]{3,1,2,0:T(8,128)} copy(f32[128,8,4,512]{3,2,1,0:T(4,128)} %bitcast.95) | data formatting | bytes 16777216
  531.8 80.5 %fusion = f32[1024,2,2048]{2,0,1:T(8,128)} fusion(bf16[2,2048,8192]{2,1,0:T(8,128)(2,1)} %bitcast.2, bf16[1024,8192]{1,0:T(8,128)(2,1)} %all-gather.2.cloned.1.call-done), kind=kOutput, calls=%fused_computation.7 | convolution fusion | flops 68719476736 | bytes 100663296 | tf_op jit(solution)/shard_map/dot_general | solution.py:55
  612.3 14.8 %fusion.4 = bf16[1024,2048]{1,0:T(8,128)(2,1)} fusion(f32[1024,2048]{1,0:T(8,128)} %bitcast.96, f32[1024,2,2048]{2,0,1:T(8,128)} %fusion, f32[1024,2048]{1,0:T(8,128)} %bitcast.97), kind=kLoop, calls=%fused_computation.12 | loop fusion | flops 16777216 | bytes 37748736 | tf_op jit(solution)/shard_map/convert_element_type | solution.py:93
  (33 shorter events, 6.4 us)
Async XLA Ops:
  6.5 21.4 %copy-start = (s32[8]{0:T(128)S(1)}, s32[8]{0:T(128)}, u32[]{:S(2)}) copy-start(s32[8]{0:T(128)} %param.13) | copy-start | bytes 100
  10.5 17.3 %copy-start.4 = (s32[4,3]{1,0:T(4,128)S(1)}, s32[4,3]{1,0:T(4,128)}, u32[]{:S(2)}) copy-start(s32[4,3]{1,0:T(4,128)} %param.11) | copy-start | bytes 148
  18.4 10.4 %copy-start.3 = (bf16[1,1,8,128,1024]{4,3,2,1,0:T(8,128)(2,1)S(1)}, bf16[1,1,8,128,1024]{4,3,2,1,0:T(8,128)(2,1)}, u32[]{:S(2)}) copy-start(bf16[1,1,8,128,1024]{4,3,2,1,0:T(8,128)(2,1)} %param.10) | copy-start | bytes 6291460
  20.3 33.2 %all-to-all-start = ((bf16[8,2,32768]{2,1,0:T(2,128)(2,1)}), bf16[8,2,32768]{2,1,0:T(2,128)(2,1)S(1)}, u32[]{:S(2)}, u32[]{:S(2)}) async-start(bf16[8,2,32768]{2,1,0:T(2,128)(2,1)} %reshape.206), calls=%async_computation | async-start | bytes 2097152 | tf_op jit(solution)/shard_map/all_to_all | solution.py:42
  53.5 1.0 copy-start.2
  54.5 52.0 %all-to-all-start.2 = ((bf16[8,2,65536]{2,1,0:T(2,128)(2,1)}), bf16[8,2,65536]{2,1,0:T(2,128)(2,1)S(1)}, u32[]{:S(2)}, u32[]{:S(2)}) async-start(bf16[8,2,65536]{2,1,0:T(2,128)(2,1)} %reshape.204), calls=%async_computation.2 | async-start | bytes 4194304 | tf_op jit(solution)/shard_map/all_to_all | solution.py:43
  106.5 30.8 %all-to-all-start.1 = ((bf16[4,3,1,65536]{3,1,2,0:T(4,128)(2,1)}), bf16[4,3,1,65536]{3,1,2,0:T(4,128)(2,1)}, u32[]{:S(2)}, u32[]{:S(2)}) async-start(bf16[4,3,1,65536]{3,1,2,0:T(4,128)(2,1)} %select_bitcast_fusion), calls=%async_computation.1 | async-start | bytes 4194304 | tf_op jit(solution)/shard_map/all_to_all | solution.py:49
  137.3 5.7 copy-start.5
  137.3 150.9 %all-to-all-start.3 = ((bf16[4,3,1,131072]{3,1,2,0:T(4,128)(2,1)}), bf16[4,3,1,131072]{3,1,2,0:T(4,128)(2,1)}, u32[]{:S(2)}, u32[]{:S(2)}) async-start(bf16[4,3,1,131072]{3,1,2,0:T(4,128)(2,1)} %fusion.8), calls=%async_computation.3 | async-start | bytes 8388608 | tf_op jit(solution)/shard_map/all_to_all | solution.py:50
  142.3 229.8 %all-gather.2.cloned.1.call-start = ((), (), s32[]{:S(2)}) async-start(), calls=%async_computation.4 | async-start | bytes 18874368 | tf_op jit(solution)/shard_map/all_gather | solution.py:54
  612.3 14.8 %copy-start.1 = (s32[8]{0:T(128)S(1)}, s32[8]{0:T(128)}, u32[]{:S(2)}) copy-start(s32[8]{0:T(128)} %param.13) | copy-start | bytes 100
Sparse Core Ops, SparseCore 0:
  145.3 226.8 all-gather.1
where the time goes:
time: 644 us; the launch traced here: 634 us
  local copies, waits for them, and re-layouts  299 us (46%)
  matrix products  97.5 us (15%)
  waiting for transfers between devices  71.2 us (11%)
  blocking collectives  70 us (11%)
  other arithmetic  61.6 us (10%)
  starting transfers between devices  21.2 us (3%)
  between operations  13.8 us (2%)
    unnamed x23, local copies, waits for them, and re-layouts  101 us
    dot_general x1, local copies, waits for them, and re-layouts, per_device(): jnp.dot(gathered, gate_up_weight.reshape(full_width, 2 * local_hidden_wid...  83.4 us
    dot_general x1, matrix products, per_device(): jnp.dot(gathered, gate_up_weight.reshape(full_width, 2 * local_hidden_wid...  80.5 us
    psum x1, blocking collectives, per_device(): lax.psum(partial_shrink, ('tp', 'cores')).astype(jnp.bfloat16)  70 us
    all_gather x1, waiting for transfers between devices, per_device(): gathered = lax.all_gather(tokens, ('tp', 'cores'), axis=1, tiled=True)  37.6 us
    all_to_all x1, waiting for transfers between devices, per_device(): lax.all_to_all(local_up_factor, ('tp', 'cores'), split_axis=1, concat_axi...  28.9 us
    unnamed x3, other arithmetic  28.6 us
    gather x4, local copies, waits for them, and re-layouts, per_device(): jnp.take(b_chosen, tile_seg, axis=0)  24.6 us
  transfers between devices with their start and end apart: 5, of which 3 were waited for; matrix products, arithmetic and copies ran while one was open for 41% of the time, Pallas kernels for 0%

commit v1 on v0

--- a/solution.py
+++ b/solution.py
@@ -70,7 +70,7 @@
     partial_shrink = jnp.einsum(
         "tkd,tdr->tkr", own_features, a_tiles, preferred_element_type=jnp.float32
     )
-    reduced_input = lax.psum(partial_shrink, ("tp", "cores")).astype(jnp.bfloat16)
+    reduced_input = lax.psum(lax.psum(partial_shrink, "cores"), "tp").astype(jnp.bfloat16)
     b_tiles = jnp.take(b_chosen, tile_seg, axis=0).reshape(tile_count, groups, rank_size, 2, narrow)
     gate_adapter_delta = jnp.einsum(
         "tkr,tmrw->tkmw",

time: 644 us -> 615 us (0.955)
  blocking collectives: 70 us -> 42.3 us
    psum x1, blocking collectives: 70 us -> 42.3 us  [per_device(): lax.psum(lax.psum(partial_shrink, 'cores'), 'tp').astype(jnp.bfloat16)]
    unnamed x23 -> x27, local copies, waits for them, and re-layouts: 101 us -> 102 us
    unnamed x3 -> x4, other arithmetic: 28.6 us -> 28.7 us
  transfers between devices with their start and end apart: 5 -> 6, of which waited for: 3 -> 3; matrix products, arithmetic and copies ran while one was open for 41% -> 56% of each run, Pallas kernels for 0% -> 0%
where the time goes in v1:
time: 615 us; the launch traced here: 606 us
  local copies, waits for them, and re-layouts  299 us (49%)
  matrix products  99.1 us (16%)
  waiting for transfers between devices  70.7 us (11%)
  other arithmetic  59.1 us (10%)
  blocking collectives  42.3 us (7%)
  starting transfers between devices  21.2 us (3%)
  between operations  13.8 us (2%)
    unnamed x27, local copies, waits for them, and re-layouts  102 us
    dot_general x1, local copies, waits for them, and re-layouts, per_device(): jnp.dot(gathered, gate_up_weight.reshape(full_width, 2 * local_hidden_wid...  83.4 us
    dot_general x1, matrix products, per_device(): jnp.dot(gathered, gate_up_weight.reshape(full_width, 2 * local_hidden_wid...  80.9 us
    psum x1, blocking collectives, per_device(): lax.psum(lax.psum(partial_shrink, 'cores'), 'tp').astype(jnp.bfloat16)  42.3 us
    all_gather x1, waiting for transfers between devices, per_device(): gathered = lax.all_gather(tokens, ('tp', 'cores'), axis=1, tiled=True)  36.7 us
    all_to_all x1, waiting for transfers between devices, per_device(): lax.all_to_all(local_up_factor, ('tp', 'cores'), split_axis=1, concat_axi...  28.9 us
    unnamed x4, other arithmetic  28.7 us
    gather x4, local copies, waits for them, and re-layouts, per_device(): jnp.take(b_chosen, tile_seg, axis=0)  24.6 us
  transfers between devices with their start and end apart: 6, of which 3 were waited for; matrix products, arithmetic and copies ran while one was open for 56% of the time, Pallas kernels for 0%

profile of v1, /device:TPU:0, one launch (start us, length us, event | category | flops | bytes accessed | tf_op | source)
XLA Modules:
  0.0 605.5 jit_solution(7252636595005820982)
XLA Ops:
  6.5 4.0 reshape.199
  11.1 7.3 %reduce.3 = bf16[8,65536]{1,0:T(8,128)(2,1)S(1)} reduce(bf16[8,1,65536]{2,1,0:T(2,128)(2,1)S(1)} %bitcast.108, bf16[]{:T(256)} %broadcast.154), dimensions={1}, to_apply=%bitcast.85.reduce_sub_computation | reduce | bytes 2097154
  18.4 1.9 reshape.206
  20.2 7.5 %all-to-all-start = ((bf16[8,2,32768]{2,1,0:T(2,128)(2,1)}), bf16[8,2,32768]{2,1,0:T(2,128)(2,1)S(1)}, u32[]{:S(2)}, u32[]{:S(2)}) async-start(bf16[8,2,32768]{2,1,0:T(2,128)(2,1)} %reshape.206), calls=%async_computation | async-start | bytes 2097152 | tf_op jit(solution)/shard_map/all_to_all | solution.py:42
  28.7 4.1 reshape.200
  32.9 13.0 %reduce.2 = bf16[8,131072]{1,0:T(8,128)(2,1)S(1)} reduce(bf16[8,1,131072]{2,1,0:T(2,128)(2,1)} %bitcast.102, bf16[]{:T(256)} %broadcast.154), dimensions={1}, to_apply=%bitcast.83.reduce_sub_computation | reduce | bytes 4194306
  45.9 3.2 reshape.204
  49.0 4.4 all-to-all-done
  54.5 3.6 all-to-all-start.2
  58.1 5.8 reshape.207
  63.9 2.7 copy.81
  66.6 3.0 gather_fusion.1
  69.6 4.2 reshape.131
  73.8 3.9 select_bitcast_fusion
  77.6 28.9 %all-to-all-done.2 = bf16[8,2,65536]{2,1,0:T(2,128)(2,1)S(1)} async-done(((bf16[8,2,65536]{2,1,0:T(2,128)(2,1)}), bf16[8,2,65536]{2,1,0:T(2,128)(2,1)S(1)}, u32[]{:S(2)}, u32[]{:S(2)}) %all-to-all-start.2) | async-done | bytes 2097184 | tf_op jit(solution)/shard_map/all_to_all | solution.py:43
  106.5 4.7 all-to-all-start.1
  111.2 4.3 reshape.205
  115.5 4.5 copy.79
  120.1 3.0 gather_fusion.3
  123.1 4.2 reshape.149
  128.9 2.6 reshape.159
  131.5 5.8 fusion.8
  137.3 5.0 all-to-all-start.3
  143.7 45.6 %copy.69 = bf16[1024,8,2,2048]{3,1,2,0:T(8,128)(2,1)} copy(bf16[1024,8,2,2048]{3,2,1,0:T(2,128)(2,1)} %bitcast.33) | data formatting | bytes 134217728
  189.3 83.4 %copy.48 = bf16[4096,8192]{1,0:T(8,128)(2,1)} copy(bf16[4096,8192]{0,1:T(8,128)(2,1)} %bitcast.1) | data formatting | bytes 134217728 | tf_op jit(solution)/shard_map/dot_general | solution.py:55
  272.8 3.1 copy.80
  275.9 5.4 gather_fusion.2
  281.3 7.9 %gather.27 = bf16[8,1024,256]{2,1,0:T(8,128)(2,1)} reshape(bf16[8,4,65536]{2,1,0:T(4,128)(2,1)} %gather_fusion.2) | data formatting | bytes 8388608 | tf_op jit(solution)/shard_map/jit(_take)/gather | solution.py:63
  289.2 5.2 copy.78
  295.5 5.4 gather_fusion.5
  300.9 5.5 gather_fusion.6
  306.4 8.4 %pad_maximum_fusion = bf16[8,4,131072]{2,1,0:T(4,128)(2,1)} fusion(bf16[8,4,65536]{2,1,0:T(4,128)(2,1)} %gather_fusion.6, bf16[8,4,65536]{2,1,0:T(4,128)(2,1)} %gather_fusion.5), kind=kLoop, calls=%fused_computation.15 | loop fusion | flops 16777216 | bytes 16777216
  314.8 12.6 %reshape.201 = bf16[8,4,128,2,512]{4,3,2,1,0:T(2,128)(2,1)} reshape(bf16[8,4,131072]{2,1,0:T(4,128)(2,1)} %pad_maximum_fusion) | data formatting | bytes 16777216 | tf_op jit(solution)/shard_map/jit(_take)/gather | solution.py:74
  327.4 8.1 %copy_select_fusion = bf16[8,4,128,2,512]{4,2,1,0,3:T(8,128)(2,1)} fusion(bf16[8,4,128,2,512]{4,3,2,1,0:T(2,128)(2,1)} %reshape.201, pred[8]{0:T(512)(128)(4,1)S(1)} %compare_and_fusion.1), kind=kLoop, calls=%fused_computation.16 | loop fusion | flops 4194304 | bytes 16777224 | tf_op jit(solution)/shard_map/jit(_take)/select_n | solution.py:74
  335.4 36.7 %all-gather.2.cloned.1.call-done = bf16[1024,8192]{1,0:T(8,128)(2,1)} async-done(((bf16[1024,1024]{1,0:T(8,128)(2,1)}), bf16[1024,8192]{1,0:T(8,128)(2,1)}) %all-gather.2.cloned.1.call-update) | async-done | bytes 16777232 | tf_op jit(solution)/shard_map/all_gather | solution.py:54
  372.1 10.3 %copy.70 = bf16[128,8,32,256]{3,2,1,0:T(8,128)(2,1)S(1)} copy(bf16[128,8,32,256]{3,1,2,0:T(8,128)(2,1)} %bitcast.104) | data formatting | bytes 33554432
  382.4 13.7 %dynamic-slice_reduce_fusion = bf16[1024,4,256]{2,1,0:T(4,128)(2,1)S(1)} fusion(bf16[1024,4,8,256]{3,2,1,0:T(8,128)(2,1)S(1)} %bitcast.100, s32[]{:T(128)S(6)} %select_n.80), kind=kLoop, calls=%fused_computation.27 | loop fusion | bytes 4194308 | tf_op jit(solution)/shard_map/dynamic_slice | solution.py:66
  396.1 2.7 reshape.202
  398.8 4.8 fusion.9
  403.7 80.9 %fusion = f32[1024,2,2048]{2,0,1:T(8,128)} fusion(bf16[2,2048,8192]{2,1,0:T(8,128)(2,1)} %bitcast.2, bf16[1024,8192]{1,0:T(8,128)(2,1)} %all-gather.2.cloned.1.call-done), kind=kOutput, calls=%fused_computation.7 | convolution fusion | flops 68719476736 | bytes 100663296 | tf_op jit(solution)/shard_map/dot_general | solution.py:55
  484.6 42.3 %all-reduce.4 = bf16[8,128,256]{2,1,0:T(8,128)(2,1)S(1)} all-reduce(f32[8,128,256]{2,1,0:T(8,128)} %all-reduce.3.cloned.1.call-done), channel_id=1, replica_groups=mesh['grp'=4,'tp'=4,'cores'=2] {'tp'}, use_global_device_ids=true, to_apply=%region_3.4 | all-reduce | flops 262144 | bytes 1572864 | tf_op jit(solution)/shard_map/psum | solution.py:73
  526.9 6.7 %broadcast_multiply_fusion.1 = f32[8,128,4,512]{3,1,2,0:T(8,128)} fusion(bf16[8,4,128,2,512]{4,2,1,0,3:T(8,128)(2,1)} %copy_select_fusion, bf16[8,128,256]{2,1,0:T(8,128)(2,1)S(1)} %all-reduce.4), kind=kOutput, calls=%fused_computation.24 | convolution fusion | flops 538968064 | bytes 12845056 | tf_op jit(solution)/shard_map/tkr,tmrw->tkmw/dot_general | solution.py:75
  533.5 6.7 %broadcast_multiply_fusion = f32[8,128,4,512]{3,1,2,0:T(8,128)} fusion(bf16[8,4,128,2,512]{4,2,1,0,3:T(8,128)(2,1)} %copy_select_fusion, bf16[8,128,256]{2,1,0:T(8,128)(2,1)S(1)} %all-reduce.4), kind=kOutput, calls=%fused_computation.23 | convolution fusion | flops 538968064 | bytes 12845056 | tf_op jit(solution)/shard_map/tkr,tmrw->tkmw/dot_general | solution.py:81
  540.2 12.0 %copy.60 = f32[8,128,4,512]{3,2,1,0:T(4,128)} copy(f32[8,128,4,512]{3,1,2,0:T(8,128)} %broadcast_multiply_fusion) | data formatting | bytes 16777216 | tf_op jit(solution)/shard_map/mul | solution.py:90
  552.2 10.9 %copy.72 = f32[128,8,4,512]{3,1,2,0:T(8,128)} copy(f32[128,8,4,512]{3,2,1,0:T(4,128)} %bitcast.94) | data formatting | bytes 16777216
  563.1 12.0 %copy.59 = f32[8,128,4,512]{3,2,1,0:T(4,128)} copy(f32[8,128,4,512]{3,1,2,0:T(8,128)} %broadcast_multiply_fusion.1) | data formatting | bytes 16777216 | tf_op jit(solution)/shard_map/mul | solution.py:87
  575.1 11.0 %copy.71 = f32[128,8,4,512]{3,1,2,0:T(8,128)} copy(f32[128,8,4,512]{3,2,1,0:T(4,128)} %bitcast.95) | data formatting | bytes 16777216
  586.0 12.4 %fusion.4 = bf16[1024,2048]{1,0:T(8,128)(2,1)} fusion(f32[1024,2048]{1,0:T(8,128)S(1)} %bitcast.98, f32[1024,2,2048]{2,0,1:T(8,128)} %fusion, f32[1024,2048]{1,0:T(8,128)} %bitcast.99), kind=kLoop, calls=%fused_computation.12 | loop fusion | flops 16777216 | bytes 37748736 | tf_op jit(solution)/shard_map/convert_element_type | solution.py:93
  (41 shorter events, 6.8 us)
Async XLA Ops:
  6.5 21.3 %copy-start = (s32[8]{0:T(128)S(1)}, s32[8]{0:T(128)}, u32[]{:S(2)}) copy-start(s32[8]{0:T(128)} %param.13) | copy-start | bytes 100
  10.5 17.2 %copy-start.4 = (s32[4,3]{1,0:T(4,128)S(1)}, s32[4,3]{1,0:T(4,128)}, u32[]{:S(2)}) copy-start(s32[4,3]{1,0:T(4,128)} %param.11) | copy-start | bytes 148
  18.4 10.4 %copy-start.3 = (bf16[1,1,8,128,1024]{4,3,2,1,0:T(8,128)(2,1)S(1)}, bf16[1,1,8,128,1024]{4,3,2,1,0:T(8,128)(2,1)}, u32[]{:S(2)}) copy-start(bf16[1,1,8,128,1024]{4,3,2,1,0:T(8,128)(2,1)} %param.10) | copy-start | bytes 6291460
  20.2 33.2 %all-to-all-start = ((bf16[8,2,32768]{2,1,0:T(2,128)(2,1)}), bf16[8,2,32768]{2,1,0:T(2,128)(2,1)S(1)}, u32[]{:S(2)}, u32[]{:S(2)}) async-start(bf16[8,2,32768]{2,1,0:T(2,128)(2,1)} %reshape.206), calls=%async_computation | async-start | bytes 2097152 | tf_op jit(solution)/shard_map/all_to_all | solution.py:42
  53.5 1.0 copy-start.2
  54.5 52.0 %all-to-all-start.2 = ((bf16[8,2,65536]{2,1,0:T(2,128)(2,1)}), bf16[8,2,65536]{2,1,0:T(2,128)(2,1)S(1)}, u32[]{:S(2)}, u32[]{:S(2)}) async-start(bf16[8,2,65536]{2,1,0:T(2,128)(2,1)} %reshape.204), calls=%async_computation.2 | async-start | bytes 4194304 | tf_op jit(solution)/shard_map/all_to_all | solution.py:43
  106.5 30.8 %all-to-all-start.1 = ((bf16[4,3,1,65536]{3,1,2,0:T(4,128)(2,1)}), bf16[4,3,1,65536]{3,1,2,0:T(4,128)(2,1)}, u32[]{:S(2)}, u32[]{:S(2)}) async-start(bf16[4,3,1,65536]{3,1,2,0:T(4,128)(2,1)} %select_bitcast_fusion), calls=%async_computation.1 | async-start | bytes 4194304 | tf_op jit(solution)/shard_map/all_to_all | solution.py:49
  137.3 6.2 %copy-start.5 = (s32[1,3]{1,0:T(1,128)S(1)}, s32[1,3]{1,0:T(1,128)}, u32[]{:S(2)}) copy-start(s32[1,3]{1,0:T(1,128)} %param.12) | copy-start | bytes 40
  137.3 151.9 %all-to-all-start.3 = ((bf16[4,3,1,131072]{3,1,2,0:T(4,128)(2,1)}), bf16[4,3,1,131072]{3,1,2,0:T(4,128)(2,1)}, u32[]{:S(2)}, u32[]{:S(2)}) async-start(bf16[4,3,1,131072]{3,1,2,0:T(4,128)(2,1)} %fusion.8), calls=%async_computation.3 | async-start | bytes 8388608 | tf_op jit(solution)/shard_map/all_to_all | solution.py:50
  142.3 229.8 %all-gather.2.cloned.1.call-start = ((), (), s32[]{:S(2)}) async-start(), calls=%async_computation.4 | async-start | bytes 18874368 | tf_op jit(solution)/shard_map/all_gather | solution.py:54
  143.0 341.5 %all-reduce.3.cloned.1.call-start = ((), (), s32[]{:S(2)}) async-start(), calls=%async_computation.5 | async-start | bytes 2097152 | tf_op jit(solution)/shard_map/psum | solution.py:73
  575.1 11.0 %slice-start = ((s8[8388608]{0:T(1024)(128)(4,1)}), s8[4194304]{0:T(1024)(128)(4,1)S(1)}, s32[]{:S(2)}) async-start(s8[8388608]{0:T(1024)(128)(4,1)} %bitcast.96), calls=%async_computation.6 | async-start | bytes 8388608
  575.1 11.0 %slice-start.1 = ((s8[8388608]{0:T(1024)(128)(4,1)}), s8[4194304]{0:T(1024)(128)(4,1)S(1)}, s32[]{:S(2)}) async-start(s8[8388608]{0:T(1024)(128)(4,1)} %bitcast.96), calls=%async_computation.7 | async-start | bytes 8388608
  586.0 12.4 %copy-start.1 = (s32[8]{0:T(128)S(1)}, s32[8]{0:T(128)}, u32[]{:S(2)}) copy-start(s32[8]{0:T(128)} %param.13) | copy-start | bytes 100
Sparse Core Ops, SparseCore 0:
  145.3 226.7 all-gather.1
  403.8 38.2 all-reduce.2
